TPU v7x, 128 devices: a whole 4x4x4 slice. The times are simulated.
128 devices in a mesh: row: 8 (over x, core), col: 16 (over y, z).
Axes of the slice: x: 4, y: 4, z: 4, core: 2. Of those that a mesh axis runs over, the one named last changes fastest.
Arguments:
- left_factor: bfloat16 [4, 2048, 24, 4096], P(None, 'row', None, 'col'), may hold values from -0.01953125 to 0.01953125
- prev_solution: bfloat16 [24, 4096, 512], P('row', 'col'), may hold values from -6 to 6
- cross: bfloat16 [4, 2048, 512], P(None, 'row'), may hold values from -6 to 6
- inverses: bfloat16 [2, 2, 2048, 1, 4096], P(None, None, 'row', None, 'col'), as said below
- coupling: bfloat16 [2, 2048, 1, 4096], P(None, 'row', None, 'col'), may hold values from -0.09375 to 0.09375
- prior_cov: float32 [512, 512], P('col'), may hold values from -6 to 6
Outputs:
- solved: bfloat16 [4, 2048, 512], P(None, 'row')
- pred_cov: float32 [512, 512], P('col')
Inputs may be any that keep to these rules, and one draw needn't show every extreme that they name: Each block of inverses is lower triangular in natural order, with diagonal entries from 0.5 to 1.5.
All inputs are finite; a program needn't handle non-finite values.
Results may differ from a plain program's by a relative error of at most 0.0056.
Values may be sent and summed in bfloat16 or wider, within the bound.
No kernel may reach another device: no remote copies, remote signals or barrier semaphores. Data moves between devices by JAX's collectives and lax.ppermute only.
A program may use at most 64 MiB of HBM per device.

v0:
```python
import jax
import jax.numpy as jnp
from jax import lax
from jax.sharding import PartitionSpec as P

S = 8192


def from_root(shard, axis, root):
    return lax.dynamic_index_in_dim(lax.all_gather(shard, axis), root, 0, keepdims=False)


def filled_up(lines, peers):
    spare = -len(lines) % peers
    return jnp.pad(lines, [(0, spare)] + [(0, 0)] * (lines.ndim - 1))


def in_order(blocks, dim):
    shape = list(blocks.shape[1:])
    shape[dim] *= blocks.shape[0]
    return jnp.moveaxis(blocks, 0, dim).reshape(shape)


def from_everyone(shard, axis):
    peers = lax.axis_size(axis)
    return lax.all_to_all(
        jnp.broadcast_to(shard[None], (peers, *shard.shape)), axis, 0, 0, tiled=True
    )


def gather_directly(shard, axis, dim):
    return in_order(from_everyone(shard, axis), dim)


def cut_along(shard, dim, peers):
    shape = shard.shape
    blocks = shard.reshape(*shape[:dim], peers, shape[dim] // peers, *shape[dim + 1 :])
    return jnp.moveaxis(blocks, dim, 0)


def sent_and_summed(shard, axis, dim):
    blocks = cut_along(shard, dim, lax.axis_size(axis))
    arrived = lax.all_to_all(blocks, axis, split_axis=0, concat_axis=0, tiled=True)
    return arrived.sum(axis=0)


def sum_by_parts(shard, axes):
    lines = shard.reshape(-1, shard.shape[-1])
    padded = filled_up(lines, lax.axis_size(axes))
    whole = gather_directly(sent_and_summed(padded, axes, 0), axes, 0)
    return lax.slice_in_dim(whole, 0, len(lines)).reshape(shard.shape)


def over_copies(shard, axis):
    return from_everyone(shard, axis).astype(jnp.float32).sum(axis=0)


def apply_block(matrix, values):
    return jnp.einsum("atbu,bum->atm", matrix, values, preferred_element_type=jnp.float32)


def spread_rows(values):
    n_row = lax.axis_size("row")
    n_col = lax.axis_size("col")
    col_id = lax.axis_index("col")
    rounds, tile, sites = values.shape
    group = n_col // n_row
    grouped = values.reshape(rounds // group, group, tile, sites)
    picked = lax.dynamic_index_in_dim(grouped, col_id // n_row, 1, keepdims=False)
    return from_root(picked, "row", col_id % n_row)


def column_sum(values):
    return sum_by_parts(values, "col")


def solve_rounded(values):
    return sum_by_parts(values, "col").astype(jnp.bfloat16)


def outer_rows(solution):
    share = solution.shape[2] // lax.axis_size("col")
    own = lax.dynamic_slice_in_dim(solution, lax.axis_index("col") * share, share, 2)
    return jnp.einsum("atm,atn->mn", own, solution, preferred_element_type=jnp.float32)


def body(left_factor, prev_solution, cross, inverses, coupling, prior_cov):
    half = coupling.shape[0]
    pre = jnp.einsum(
        "atbu,bum->atm",
        left_factor,
        lax.all_gather(prev_solution, "row", axis=0, tiled=True),
        preferred_element_type=jnp.float32,
    )
    cross_first = cross[:half].astype(jnp.float32)
    cross_second = cross[half:].astype(jnp.float32)
    pre_first = sum_by_parts(pre[:half], "col")
    first_rhs = (cross_first - pre_first).astype(jnp.bfloat16)
    solved_first = solve_rounded(apply_block(inverses[0], spread_rows(first_rhs)))
    linked = column_sum(pre[half:] + apply_block(coupling, spread_rows(solved_first)))
    second_rhs = (cross_second - linked).astype(jnp.bfloat16)
    solved_second = solve_rounded(apply_block(inverses[1], spread_rows(second_rhs)))
    solved_all = jnp.concatenate([solved_first, solved_second], axis=0)
    outer_total = over_copies(outer_rows(solved_all).astype(jnp.bfloat16), "row").astype(
        jnp.float32
    )
    pred_cov = prior_cov - outer_total / S
    return (solved_all, pred_cov)


def solution(mesh):
    placed = (
        P(None, "row", None, "col"),
        P("row", "col", None),
        P(None, "row", None),
        P(None, None, "row", None, "col"),
        P(None, "row", None, "col"),
        P("col", None),
    )
    return jax.shard_map(
        body,
        mesh=mesh,
        in_specs=placed,
        out_specs=(P(None, "row", None), P("col", None)),
        check_vma=False,
    )
```

profile of v0, /device:TPU:1, one launch (start us, length us, event | category | flops | bytes accessed | tf_op | source)
XLA Modules:
  0.0 326.6 jit_solution(15073894378876235162)
XLA Ops:
  7.2 0.0 copy-start
  7.2 0.0 all-gather.8.cloned.1.call-start
  7.2 0.7 all-gather.8.cloned.1.call-update
  7.9 46.3 %all-gather.8.cloned.1.call-done = bf16[24,256,512]{2,1,0:T(8,128)(2,1)} async-done(((bf16[3,256,512]{2,1,0:T(8,128)(2,1)}), bf16[24,256,512]{2,1,0:T(8,128)(2,1)}) %all-gather.8.cloned.1.call-update) | async-done | bytes 6291472 | tf_op jit(solution)/shard_map/all_gather | solution.py:92
  54.2 14.2 %fusion.3 = f32[4,256,512]{2,1,0:T(8,128)S(1)} fusion(bf16[24,256,512]{2,1,0:T(8,128)(2,1)} %all-gather.8.cloned.1.call-done, bf16[4,256,24,256]{3,2,1,0:T(8,128)(2,1)} %param.6), kind=kOutput, calls=%fused_computation.3 | convolution fusion | flops 6442450944 | bytes 20971520 | tf_op jit(solution)/shard_map/atbu,bum->atm/dot_general | solution.py:89
  68.4 0.1 slice.24
  68.5 22.4 %all_to_all.45 = f32[16,32,512]{2,1,0:T(8,128)S(1)} all-to-all(f32[16,32,512]{2,1,0:T(8,128)S(1)} %bitcast.52), channel_id=1, replica_groups=mesh['row'=8,'col'=16] {'col'}, dimensions={0} | all-to-all | bytes 2097152 | tf_op jit(solution)/shard_map/all_to_all | solution.py:43
  90.9 0.1 reduce_sum.45
  91.0 1.1 broadcast_in_dim.10
  92.1 3.9 %all-to-all-start.1 = ((f32[16,32,512]{2,1,0:T(8,128)}), f32[16,32,512]{2,1,0:T(8,128)S(1)}, u32[]{:S(2)}, u32[]{:S(2)}) async-start(f32[16,32,512]{2,1,0:T(8,128)} %broadcast_in_dim.10), calls=%async_computation.1 | async-start | bytes 2097152 | tf_op jit(solution)/shard_map/all_to_all | solution.py:26
  96.0 0.0 all-gather.10.cloned.1.call-start
  96.1 2.3 fusion.26
  98.4 12.7 %all-to-all-done.1 = f32[16,32,512]{2,1,0:T(8,128)S(1)} async-done(((f32[16,32,512]{2,1,0:T(8,128)}), f32[16,32,512]{2,1,0:T(8,128)S(1)}, u32[]{:S(2)}, u32[]{:S(2)}) %all-to-all-start.1) | async-done | bytes 1048608 | tf_op jit(solution)/shard_map/all_to_all | solution.py:26
  111.0 1.7 fusion.11
  112.8 0.0 all-gather.10.cloned.1.call-update
  112.8 0.0 all-gather.12.cloned.1.call-start
  112.9 1.8 fusion.27
  114.6 22.8 %all-gather.10.cloned.1.call-done = bf16[8,256,512]{2,1,0:T(8,128)(2,1)} async-done(((bf16[1,256,512]{2,1,0:T(8,128)(2,1)}), bf16[8,256,512]{2,1,0:T(8,128)(2,1)}) %all-gather.10.cloned.1.call-update) | async-done | bytes 2097168 | tf_op jit(solution)/shard_map/all_gather | solution.py:10
  137.5 1.2 convolution_bitcast_fusion.2
  138.7 22.4 %all_to_all.46 = f32[16,32,512]{2,1,0:T(8,128)S(1)} all-to-all(f32[16,32,512]{2,1,0:T(8,128)S(1)} %convolution_bitcast_fusion.2), channel_id=1, replica_groups=mesh['row'=8,'col'=16] {'col'}, dimensions={0} | all-to-all | bytes 2097152 | tf_op jit(solution)/shard_map/all_to_all | solution.py:43
  161.1 0.1 reduce_sum.46
  161.3 12.8 %all_to_all.47 = bf16[16,32,512]{2,1,0:T(8,128)(2,1)S(1)} all-to-all(bf16[16,32,512]{2,1,0:T(8,128)(2,1)S(1)} %broadcast_in_dim.11), channel_id=1, replica_groups=mesh['row'=8,'col'=16] {'col'}, dimensions={0} | all-to-all | bytes 1048576 | tf_op jit(solution)/shard_map/all_to_all | solution.py:26
  174.0 0.7 constant_dynamic-slice_fusion
  174.7 0.0 all-gather.12.cloned.1.call-update
  174.8 0.0 all-gather.14.cloned.1.call-start
  174.8 25.1 %all-gather.12.cloned.1.call-done = bf16[8,256,512]{2,1,0:T(8,128)(2,1)} async-done(((bf16[1,256,512]{2,1,0:T(8,128)(2,1)}), bf16[8,256,512]{2,1,0:T(8,128)(2,1)}) %all-gather.12.cloned.1.call-update) | async-done | bytes 2097168 | tf_op jit(solution)/shard_map/all_gather | solution.py:10
  199.9 0.0 copy-done
  199.9 1.2 fusion.8
  201.2 22.4 %all_to_all.48 = f32[16,32,512]{2,1,0:T(8,128)S(1)} all-to-all(f32[16,32,512]{2,1,0:T(8,128)S(1)} %bitcast.51), channel_id=1, replica_groups=mesh['row'=8,'col'=16] {'col'}, dimensions={0} | all-to-all | bytes 2097152 | tf_op jit(solution)/shard_map/all_to_all | solution.py:43
  223.6 0.0 copy-start.2
  223.6 0.1 reduce_sum.47
  223.7 0.0 copy-start.3
  223.7 0.1 broadcast_in_dim.12
  223.8 18.5 %all_to_all.49 = f32[16,32,512]{2,1,0:T(8,128)S(1)} all-to-all(f32[16,32,512]{2,1,0:T(8,128)S(1)} %broadcast_in_dim.12), channel_id=1, replica_groups=mesh['row'=8,'col'=16] {'col'}, dimensions={0} | all-to-all | bytes 2097152 | tf_op jit(solution)/shard_map/all_to_all | solution.py:26
  242.3 0.0 copy-done.2
  242.3 0.8 fusion.10
  243.1 0.0 all-gather.14.cloned.1.call-update
  243.1 25.2 %all-gather.14.cloned.1.call-done = bf16[8,256,512]{2,1,0:T(8,128)(2,1)} async-done(((bf16[1,256,512]{2,1,0:T(8,128)(2,1)}), bf16[8,256,512]{2,1,0:T(8,128)(2,1)}) %all-gather.14.cloned.1.call-update) | async-done | bytes 2097168 | tf_op jit(solution)/shard_map/all_gather | solution.py:10
  268.3 0.0 copy-done.3
  268.3 1.2 convolution_bitcast_fusion
  269.6 22.4 %all_to_all.50 = f32[16,32,512]{2,1,0:T(8,128)S(1)} all-to-all(f32[16,32,512]{2,1,0:T(8,128)S(1)} %convolution_bitcast_fusion), channel_id=1, replica_groups=mesh['row'=8,'col'=16] {'col'}, dimensions={0} | all-to-all | bytes 2097152 | tf_op jit(solution)/shard_map/all_to_all | solution.py:43
  292.0 0.1 reduce_sum.48
  292.1 0.8 broadcast_in_dim.13
  292.9 3.9 %all-to-all-start.7 = ((bf16[16,32,512]{2,1,0:T(8,128)(2,1)}), bf16[16,32,512]{2,1,0:T(8,128)(2,1)S(1)}, u32[]{:S(2)}, u32[]{:S(2)}) async-start(bf16[16,32,512]{2,1,0:T(8,128)(2,1)} %broadcast_in_dim.13), calls=%async_computation.7 | async-start | bytes 1048576 | tf_op jit(solution)/shard_map/all_to_all | solution.py:26
  296.8 9.1 %all-to-all-done.7 = bf16[16,32,512]{2,1,0:T(8,128)(2,1)S(1)} async-done(((bf16[16,32,512]{2,1,0:T(8,128)(2,1)}), bf16[16,32,512]{2,1,0:T(8,128)(2,1)S(1)}, u32[]{:S(2)}, u32[]{:S(2)}) %all-to-all-start.7) | async-done | bytes 524320 | tf_op jit(solution)/shard_map/all_to_all | solution.py:26
  306.0 0.1 pad_maximum_fusion
  306.1 0.0 copy-start.1
  306.1 0.0 copy-start.4
  306.1 0.4 fusion.9
  306.6 12.9 %all_to_all.51 = bf16[8,32,512]{2,1,0:T(8,128)(2,1)S(1)} all-to-all(bf16[8,32,512]{2,1,0:T(8,128)(2,1)S(1)} %broadcast_in_dim.14), channel_id=1, replica_groups=mesh['row'=8,'col'=16] {'row'}, dimensions={0} | all-to-all | bytes 524288 | tf_op jit(solution)/shard_map/all_to_all | solution.py:26
  319.5 0.0 copy-done.4
  319.5 0.6 multiply_subtract_fusion
  320.1 0.0 copy-done.1
  (3 shorter events, 0.1 us)
Async XLA Ops:
  7.2 192.8 %copy-start = (bf16[2,256,1,256]{3,1,2,0:T(8,128)(2,1)S(1)}, bf16[2,256,1,256]{3,1,2,0:T(8,128)(2,1)}, u32[]{:S(2)}) copy-start(bf16[2,256,1,256]{3,1,2,0:T(8,128)(2,1)} %param.10) | copy-start | bytes 786436
  7.2 47.1 %all-gather.8.cloned.1.call-start = ((), (), s32[]{:S(2)}) async-start(), calls=%async_computation.9 | async-start | bytes 7077888 | tf_op jit(solution)/shard_map/all_gather | solution.py:92
  92.1 19.0 %all-to-all-start.1 = ((f32[16,32,512]{2,1,0:T(8,128)}), f32[16,32,512]{2,1,0:T(8,128)S(1)}, u32[]{:S(2)}, u32[]{:S(2)}) async-start(f32[16,32,512]{2,1,0:T(8,128)} %broadcast_in_dim.10), calls=%async_computation.1 | async-start | bytes 2097152 | tf_op jit(solution)/shard_map/all_to_all | solution.py:26
  96.0 41.4 %all-gather.10.cloned.1.call-start = ((), (), s32[]{:S(2)}) async-start(), calls=%async_computation.10 | async-start | bytes 2359296 | tf_op jit(solution)/shard_map/all_gather | solution.py:10
  112.8 87.1 %all-gather.12.cloned.1.call-start = ((), (), s32[]{:S(2)}) async-start(), calls=%async_computation.11 | async-start | bytes 2359296 | tf_op jit(solution)/shard_map/all_gather | solution.py:10
  174.8 93.5 %all-gather.14.cloned.1.call-start = ((), (), s32[]{:S(2)}) async-start(), calls=%async_computation.12 | async-start | bytes 2359296 | tf_op jit(solution)/shard_map/all_gather | solution.py:10
  223.6 18.7 %copy-start.2 = (bf16[2,256,512]{2,1,0:T(8,128)(2,1)S(1)}, bf16[2,256,512]{2,1,0:T(8,128)(2,1)}, u32[]{:S(2)}) copy-start(bf16[2,256,512]{2,1,0:T(8,128)(2,1)} %get-tuple-element.2) | copy-start | bytes 1572868
  223.7 44.6 %copy-start.3 = (bf16[1,2,256,1,256]{4,2,3,1,0:T(8,128)(2,1)S(1)}, bf16[1,2,256,1,256]{4,2,3,1,0:T(8,128)(2,1)}, u32[]{:S(2)}) copy-start(bf16[1,2,256,1,256]{4,2,3,1,0:T(8,128)(2,1)} %get-tuple-element.5) | copy-start | bytes 786436
  292.9 13.1 %all-to-all-start.7 = ((bf16[16,32,512]{2,1,0:T(8,128)(2,1)}), bf16[16,32,512]{2,1,0:T(8,128)(2,1)S(1)}, u32[]{:S(2)}, u32[]{:S(2)}) async-start(bf16[16,32,512]{2,1,0:T(8,128)(2,1)} %broadcast_in_dim.13), calls=%async_computation.7 | async-start | bytes 1048576 | tf_op jit(solution)/shard_map/all_to_all | solution.py:26
  306.1 14.0 %copy-start.1 = (bf16[4,256,512]{2,1,0:T(8,128)(2,1)}, bf16[4,256,512]{2,1,0:T(8,128)(2,1)S(1)}, u32[]{:S(2)}) copy-start(bf16[4,256,512]{2,1,0:T(8,128)(2,1)S(1)} %pad_maximum_fusion) | copy-start | bytes 3145732
  306.1 13.4 %copy-start.4 = (f32[32,512]{1,0:T(8,128)S(1)}, f32[32,512]{1,0:T(8,128)}, u32[]{:S(2)}) copy-start(f32[32,512]{1,0:T(8,128)} %param.11) | copy-start | bytes 196612
Sparse Core Ops, SparseCore 0:
  9.7 44.4 all-gather.7
  112.9 24.4 all-gather.9
  174.9 25.0 all-gather.11
  243.2 25.0 all-gather.13
where the time goes:
time: 327 us
  waiting for transfers between devices  142 us (43%)
  blocking collectives  134 us (41%)
  matrix products  18.3 us (6%)
  between operations  13.9 us (4%)
  starting transfers between devices  8 us (2%)
  local copies, waits for them, and re-layouts  7.02 us (2%)
  other arithmetic  3.55 us (1%)
    all_to_all x4, blocking collectives, sent_and_summed(): lax.all_to_all(blocks, axis, split_axis=0, concat_axis=0, tiled=True)  89.7 us
    all_gather x3, waiting for transfers between devices, from_root(): lax.all_gather(shard, axis)  73.1 us
    all_gather x1, waiting for transfers between devices, body(): lax.all_gather(prev_solution, 'row', axis=0, tiled=True)  46.3 us
    all_to_all x3, blocking collectives, from_everyone(): lax.all_to_all(jnp.broadcast_to(shard[None], (peers, *shard.shape)), axis...  44.1 us
    all_to_all x2, waiting for transfers between devices, from_everyone(): lax.all_to_all(jnp.broadcast_to(shard[None], (peers, *shard.shape)), axis...  21.8 us
    dot_general x1, matrix products, body(): jnp.einsum('atbu,bum->atm', left_factor, lax.all_gather(prev_solution, 'r...  14.2 us
    all_to_all x2, starting transfers between devices, from_everyone(): lax.all_to_all(jnp.broadcast_to(shard[None], (peers, *shard.shape)), axis...  7.83 us
  transfers between devices with their start and end apart: 6, of which 6 were waited for; matrix products, arithmetic and copies ran while one was open for 1% of the time, Pallas kernels for 0%

commit v1 on v0

--- a/solution.py
+++ b/solution.py
@@ -4,6 +4,22 @@
 from jax.sharding import PartitionSpec as P
 
 S = 8192
+
+
+def product_in_turn(x, axis, dim, contribution):
+    count, index, rows = (lax.axis_size(axis), lax.axis_index(axis), x.shape[dim])
+    ahead = [(i, (i + 1) % count) for i in range(count)]
+    left = [(i, (i - 1) % count) for i in range(count)]
+    half = count // 2
+    from_left = from_right = x
+    total = contribution(x, index * rows)
+    for step in range(1, half + 1):
+        from_left = lax.ppermute(from_left, axis, ahead)
+        if step < count - half:
+            from_right = lax.ppermute(from_right, axis, left)
+            total = total + contribution(from_right, (index + step) % count * rows)
+        total = total + contribution(from_left, (index - step) % count * rows)
+    return total
 
 
 def from_root(shard, axis, root):
@@ -86,11 +102,16 @@
 
 def body(left_factor, prev_solution, cross, inverses, coupling, prior_cov):
     half = coupling.shape[0]
-    pre = jnp.einsum(
-        "atbu,bum->atm",
-        left_factor,
-        lax.all_gather(prev_solution, "row", axis=0, tiled=True),
-        preferred_element_type=jnp.float32,
+    pre = product_in_turn(
+        prev_solution,
+        "row",
+        0,
+        lambda part, start: jnp.einsum(
+            "atbu,bum->atm",
+            lax.dynamic_slice_in_dim(left_factor, start, part.shape[0], axis=2),
+            part,
+            preferred_element_type=jnp.float32,
+        ),
     )
     cross_first = cross[:half].astype(jnp.float32)
     cross_second = cross[half:].astype(jnp.float32)

time: 327 us -> 341 us (1.043)
  local copies, waits for them, and re-layouts: 7.02 us -> 35.6 us
  waiting for transfers between devices: 142 us -> 122 us
  starting transfers between devices: 8 us -> 16.7 us
    all_gather x1 -> x0, waiting for transfers between devices: 46.3 us -> none  [body(): lax.all_gather(prev_solution, 'row', axis=0, tiled=True)]
    dynamic_slice x0 -> x1, local copies, waits for them, and re-layouts: none -> 27.8 us  [body(): lax.dynamic_slice_in_dim(left_factor, start, part.shape[0], axis=2)]
    ppermute x0 -> x7, waiting for transfers between devices: none -> 17.5 us  [the longest x4 9.69 us: product_in_turn(): from_left = lax.ppermute(from_left, axis, ahead)]
    all_gather x3, waiting for transfers between devices: 73.1 us -> 85.4 us  [from_root(): lax.all_gather(shard, axis)]
    ppermute x0 -> x7, starting transfers between devices: none -> 8.78 us  [the longest x4 7.99 us: product_in_turn(): from_left = lax.ppermute(from_left, axis, ahead)]
    dot_general x1 -> x8, matrix products: 14.2 us -> 13.8 us  [body(): jnp.einsum('atbu,bum->atm', lax.dynamic_slice_in_dim(left_factor, start,...]
  transfers between devices with their start and end apart: 6 -> 12, of which waited for: 6 -> 9; matrix products, arithmetic and copies ran while one was open for 1% -> 13% of each run, Pallas kernels for 0% -> 0%
where the time goes in v1:
time: 341 us; the launch traced here: 340 us
  blocking collectives  131 us (38%)
  waiting for transfers between devices  122 us (36%)
  local copies, waits for them, and re-layouts  35.6 us (10%)
  matrix products  18 us (5%)
  starting transfers between devices  16.7 us (5%)
  between operations  14 us (4%)
  other arithmetic  3.57 us (1%)
    all_to_all x4, blocking collectives, sent_and_summed(): lax.all_to_all(blocks, axis, split_axis=0, concat_axis=0, tiled=True)  86.6 us
    all_gather x3, waiting for transfers between devices, from_root(): lax.all_gather(shard, axis)  85.4 us
    all_to_all x3, blocking collectives, from_everyone(): lax.all_to_all(jnp.broadcast_to(shard[None], (peers, *shard.shape)), axis...  44 us
    dynamic_slice x1, local copies, waits for them, and re-layouts, body(): lax.dynamic_slice_in_dim(left_factor, start, part.shape[0], axis=2)  27.8 us
    all_to_all x2, waiting for transfers between devices, from_everyone(): lax.all_to_all(jnp.broadcast_to(shard[None], (peers, *shard.shape)), axis...  18.7 us
    dot_general x8, matrix products, body(): jnp.einsum('atbu,bum->atm', lax.dynamic_slice_in_dim(left_factor, start,...  13.8 us
    ppermute x4, waiting for transfers between devices, product_in_turn(): from_left = lax.ppermute(from_left, axis, ahead)  9.69 us
    ppermute x4, starting transfers between devices, product_in_turn(): from_left = lax.ppermute(from_left, axis, ahead)  7.99 us
  transfers between devices with their start and end apart: 12, of which 9 were waited for; matrix products, arithmetic and copies ran while one was open for 13% of the time, Pallas kernels for 0%

profile of v1, /device:TPU:1, one launch (start us, length us, event | category | flops | bytes accessed | tf_op | source)
XLA Modules:
  0.0 340.0 jit_solution(17009649911504501715)
XLA Ops:
  7.2 0.0 copy-start
  7.2 2.6 collective-permute-start.1
  9.8 9.2 %collective-permute-done.1 = bf16[3,256,512]{2,1,0:T(8,128)(2,1)} collective-permute-done((bf16[3,256,512]{2,1,0:T(8,128)(2,1)}, bf16[3,256,512]{2,1,0:T(8,128)(2,1)}, u32[]{:S(2)}, u32[]{:S(2)}) %collective-permute-start.1) | collective-permute-done | bytes 786464 | tf_op jit(solution)/shard_map/ppermute | solution.py:17
  19.0 2.5 collective-permute-start.3
  21.5 27.8 %constant_dynamic-slice_fusion.1 = (bf16[4,256,3,256]{3,2,1,0:T(4,128)(2,1)}, bf16[4,256,3,256]{3,2,1,0:T(4,128)(2,1)}, bf16[4,256,3,256]{3,2,1,0:T(4,128)(2,1)S...) fusion(bf16[4,256,24,256]{3,2,1,0:T(8,128)(2,1)} %param.6, ...), kind=kLoop, calls=%fused_computation.58 | loop fusion | bytes 25165856 | tf_op jit(solution)/shard_map/dynamic_slice | solution.py:111
  49.3 0.0 collective-permute-start.2
  49.4 2.7 fusion.13
  52.1 1.7 collective-permute-start.5
  53.8 2.3 fusion.11
  56.1 2.3 fusion.9
  58.4 2.9 collective-permute-done.2
  61.3 0.7 collective-permute-start.4
  62.0 2.3 fusion.5
  64.3 1.2 collective-permute-start.6
  65.5 1.0 fusion.7
  66.4 0.6 copy-done.3
  67.1 1.0 fusion.1
  68.0 4.9 %collective-permute-done.4 = bf16[3,256,512]{2,1,0:T(8,128)(2,1)S(1)} collective-permute-done((bf16[3,256,512]{2,1,0:T(8,128)(2,1)S(1)}, bf16[3,256,512]{2,1,0:T(8,128)(2,1)S(1)}, u32[]{:S(2)}, u32[]{:S(2)}) %collective-permute-start.4) | collective-permute-done | bytes 786464 | tf_op jit(solution)/shard_map/ppermute | solution.py:19
  73.0 1.0 fusion.3
  74.0 0.4 collective-permute-done.6
  74.4 0.2 copy-done.1
  74.6 1.4 bitcast_add_fusion
  76.0 0.1 slice.24
  76.1 19.3 %all_to_all.45 = f32[16,32,512]{2,1,0:T(8,128)S(1)} all-to-all(f32[16,32,512]{2,1,0:T(8,128)S(1)} %bitcast.106), channel_id=1, replica_groups=mesh['row'=8,'col'=16] {'col'}, dimensions={0} | all-to-all | bytes 2097152 | tf_op jit(solution)/shard_map/all_to_all | solution.py:59
  95.4 0.1 reduce_sum.45
  95.5 1.1 broadcast_in_dim.10
  96.6 3.7 %all-to-all-start.1 = ((f32[16,32,512]{2,1,0:T(8,128)}), f32[16,32,512]{2,1,0:T(8,128)S(1)}, u32[]{:S(2)}, u32[]{:S(2)}) async-start(f32[16,32,512]{2,1,0:T(8,128)} %broadcast_in_dim.10), calls=%async_computation.1 | async-start | bytes 2097152 | tf_op jit(solution)/shard_map/all_to_all | solution.py:42
  100.2 0.0 all-gather.7.cloned.1.call-start
  100.3 2.2 fusion.42
  102.5 9.5 %all-to-all-done.1 = f32[16,32,512]{2,1,0:T(8,128)S(1)} async-done(((f32[16,32,512]{2,1,0:T(8,128)}), f32[16,32,512]{2,1,0:T(8,128)S(1)}, u32[]{:S(2)}, u32[]{:S(2)}) %all-to-all-start.1) | async-done | bytes 1048608 | tf_op jit(solution)/shard_map/all_to_all | solution.py:42
  112.0 1.7 fusion.25
  113.8 0.0 all-gather.7.cloned.1.call-update
  113.8 0.2 all-gather.9.cloned.1.call-start
  114.1 1.8 fusion.43
  115.8 35.0 %all-gather.7.cloned.1.call-done = bf16[8,256,512]{2,1,0:T(8,128)(2,1)} async-done(((bf16[1,256,512]{2,1,0:T(8,128)(2,1)}), bf16[8,256,512]{2,1,0:T(8,128)(2,1)}) %all-gather.7.cloned.1.call-update) | async-done | bytes 2097168 | tf_op jit(solution)/shard_map/all_gather | solution.py:26
  150.8 1.2 convolution_bitcast_fusion.2
  152.1 22.4 %all_to_all.46 = f32[16,32,512]{2,1,0:T(8,128)S(1)} all-to-all(f32[16,32,512]{2,1,0:T(8,128)S(1)} %convolution_bitcast_fusion.2), channel_id=1, replica_groups=mesh['row'=8,'col'=16] {'col'}, dimensions={0} | all-to-all | bytes 2097152 | tf_op jit(solution)/shard_map/all_to_all | solution.py:59
  174.5 0.1 reduce_sum.46
  174.7 12.7 %all_to_all.47 = bf16[16,32,512]{2,1,0:T(8,128)(2,1)S(1)} all-to-all(bf16[16,32,512]{2,1,0:T(8,128)(2,1)S(1)} %broadcast_in_dim.11), channel_id=1, replica_groups=mesh['row'=8,'col'=16] {'col'}, dimensions={0} | all-to-all | bytes 1048576 | tf_op jit(solution)/shard_map/all_to_all | solution.py:42
  187.4 0.7 constant_dynamic-slice_fusion
  188.1 0.0 all-gather.9.cloned.1.call-update
  188.2 0.0 all-gather.11.cloned.1.call-start
  188.2 25.1 %all-gather.9.cloned.1.call-done = bf16[8,256,512]{2,1,0:T(8,128)(2,1)} async-done(((bf16[1,256,512]{2,1,0:T(8,128)(2,1)}), bf16[8,256,512]{2,1,0:T(8,128)(2,1)}) %all-gather.9.cloned.1.call-update) | async-done | bytes 2097168 | tf_op jit(solution)/shard_map/all_gather | solution.py:26
  213.3 1.2 slice_add_fusion
  214.6 22.4 %all_to_all.48 = f32[16,32,512]{2,1,0:T(8,128)S(1)} all-to-all(f32[16,32,512]{2,1,0:T(8,128)S(1)} %bitcast.105), channel_id=1, replica_groups=mesh['row'=8,'col'=16] {'col'}, dimensions={0} | all-to-all | bytes 2097152 | tf_op jit(solution)/shard_map/all_to_all | solution.py:59
  237.0 0.1 reduce_sum.47
  237.1 0.0 copy-start.9
  237.1 0.1 broadcast_in_dim.12
  237.2 18.5 %all_to_all.49 = f32[16,32,512]{2,1,0:T(8,128)S(1)} all-to-all(f32[16,32,512]{2,1,0:T(8,128)S(1)} %broadcast_in_dim.12), channel_id=1, replica_groups=mesh['row'=8,'col'=16] {'col'}, dimensions={0} | all-to-all | bytes 2097152 | tf_op jit(solution)/shard_map/all_to_all | solution.py:42
  255.7 0.8 fusion.24
  256.5 0.0 all-gather.11.cloned.1.call-update
  256.5 25.2 %all-gather.11.cloned.1.call-done = bf16[8,256,512]{2,1,0:T(8,128)(2,1)} async-done(((bf16[1,256,512]{2,1,0:T(8,128)(2,1)}), bf16[8,256,512]{2,1,0:T(8,128)(2,1)}) %all-gather.11.cloned.1.call-update) | async-done | bytes 2097168 | tf_op jit(solution)/shard_map/all_gather | solution.py:26
  281.7 1.2 convolution_bitcast_fusion
  283.0 22.4 %all_to_all.50 = f32[16,32,512]{2,1,0:T(8,128)S(1)} all-to-all(f32[16,32,512]{2,1,0:T(8,128)S(1)} %convolution_bitcast_fusion), channel_id=1, replica_groups=mesh['row'=8,'col'=16] {'col'}, dimensions={0} | all-to-all | bytes 2097152 | tf_op jit(solution)/shard_map/all_to_all | solution.py:59
  305.4 0.1 reduce_sum.48
  305.5 0.8 broadcast_in_dim.13
  306.3 3.9 %all-to-all-start.7 = ((bf16[16,32,512]{2,1,0:T(8,128)(2,1)}), bf16[16,32,512]{2,1,0:T(8,128)(2,1)S(1)}, u32[]{:S(2)}, u32[]{:S(2)}) async-start(bf16[16,32,512]{2,1,0:T(8,128)(2,1)} %broadcast_in_dim.13), calls=%async_computation.7 | async-start | bytes 1048576 | tf_op jit(solution)/shard_map/all_to_all | solution.py:42
  310.2 9.2 %all-to-all-done.7 = bf16[16,32,512]{2,1,0:T(8,128)(2,1)S(1)} async-done(((bf16[16,32,512]{2,1,0:T(8,128)(2,1)}), bf16[16,32,512]{2,1,0:T(8,128)(2,1)S(1)}, u32[]{:S(2)}, u32[]{:S(2)}) %all-to-all-start.7) | async-done | bytes 524320 | tf_op jit(solution)/shard_map/all_to_all | solution.py:42
  319.4 0.1 pad_maximum_fusion
  319.5 0.0 copy-start.2
  319.5 0.0 copy-start.10
  319.5 0.4 fusion.15
  320.0 12.8 %all_to_all.51 = bf16[8,32,512]{2,1,0:T(8,128)(2,1)S(1)} all-to-all(bf16[8,32,512]{2,1,0:T(8,128)(2,1)S(1)} %broadcast_in_dim.14), channel_id=1, replica_groups=mesh['row'=8,'col'=16] {'row'}, dimensions={0} | all-to-all | bytes 524288 | tf_op jit(solution)/shard_map/all_to_all | solution.py:42
  332.9 0.6 multiply_subtract_fusion
  (25 shorter events, 0.2 us)
Async XLA Ops:
  7.2 206.2 %copy-start = (bf16[2,256,1,256]{3,1,2,0:T(8,128)(2,1)S(1)}, bf16[2,256,1,256]{3,1,2,0:T(8,128)(2,1)}, u32[]{:S(2)}) copy-start(bf16[2,256,1,256]{3,1,2,0:T(8,128)(2,1)} %param.10) | copy-start | bytes 786436
  7.2 11.9 %collective-permute-start.1 = (bf16[3,256,512]{2,1,0:T(8,128)(2,1)}, bf16[3,256,512]{2,1,0:T(8,128)(2,1)}, u32[]{:S(2)}, u32[]{:S(2)}) collective-permute-start(bf16[3,256,512]{2,1,0:T(8,128)(2,1)} %param.7), channel_id=1, source_target_pairs={{0,16},{16,32},{32,48},{48,64},{64,80},{80,96},{96,112},{112,0},{1... | collective-permute-start | bytes 2359304 | tf_op jit(solution)/shard_map/ppermute | solution.py:17
  9.8 39.5 %collective-permute-start = (bf16[3,256,512]{2,1,0:T(8,128)(2,1)}, bf16[3,256,512]{2,1,0:T(8,128)(2,1)}, u32[]{:S(2)}, u32[]{:S(2)}) collective-permute-start(bf16[3,256,512]{2,1,0:T(8,128)(2,1)} %param.7), channel_id=1, source_target_pairs={{0,112},{16,0},{32,16},{48,32},{64,48},{80,64},{96,80},{112,96},{1... | collective-permute-start | bytes 2359304 | tf_op jit(solution)/shard_map/ppermute | solution.py:19
  9.8 39.6 %copy-start.11 = (bf16[3,256,512]{2,1,0:T(8,128)(2,1)S(1)}, bf16[3,256,512]{2,1,0:T(8,128)(2,1)}, u32[]{:S(2)}) copy-start(bf16[3,256,512]{2,1,0:T(8,128)(2,1)} %param.7) | copy-start | bytes 2359300
  19.0 33.1 %collective-permute-start.3 = (bf16[3,256,512]{2,1,0:T(8,128)(2,1)}, bf16[3,256,512]{2,1,0:T(8,128)(2,1)}, u32[]{:S(2)}, u32[]{:S(2)}) collective-permute-start(bf16[3,256,512]{2,1,0:T(8,128)(2,1)} %collective-permute-done.1), channel_id=1, source_target_pairs={{0,16},{16,32},{32,48},{48,64},{64,80},{80,96},{96,112},{112,0},{1... | collective-permute-start | bytes 2359304 | tf_op jit(solution)/shard_map/ppermute | solution.py:17
  49.3 11.9 %collective-permute-start.2 = (bf16[3,256,512]{2,1,0:T(8,128)(2,1)}, bf16[3,256,512]{2,1,0:T(8,128)(2,1)S(1)}, u32[]{:S(2)}, u32[]{:S(2)}) collective-permute-start(bf16[3,256,512]{2,1,0:T(8,128)(2,1)} %collective-permute-done), channel_id=1, source_target_pairs={{0,112},{16,0},{32,16},{48,32},{64,48},{80,64},{96,80},{112,96},{1... | collective-permute-start | bytes 2359304 | tf_op jit(solution)/shard_map/ppermute | solution.py:19
  49.4 4.5 %copy-start.7 = (bf16[4,256,3,256]{3,2,1,0:T(4,128)(2,1)S(1)}, bf16[4,256,3,256]{3,2,1,0:T(4,128)(2,1)}, u32[]{:S(2)}) copy-start(bf16[4,256,3,256]{3,2,1,0:T(4,128)(2,1)} %get-tuple-element.8) | copy-start | bytes 4718596
  52.1 12.2 %collective-permute-start.5 = (bf16[3,256,512]{2,1,0:T(8,128)(2,1)}, bf16[3,256,512]{2,1,0:T(8,128)(2,1)S(1)}, u32[]{:S(2)}, u32[]{:S(2)}) collective-permute-start(bf16[3,256,512]{2,1,0:T(8,128)(2,1)} %collective-permute-done.3), channel_id=1, source_target_pairs={{0,16},{16,32},{32,48},{48,64},{64,80},{80,96},{96,112},{112,0},{1... | collective-permute-start | bytes 2359304 | tf_op jit(solution)/shard_map/ppermute | solution.py:17
  53.8 2.3 copy-start.6
  56.1 5.9 %copy-start.5 = (bf16[4,256,3,256]{3,2,1,0:T(4,128)(2,1)S(1)}, bf16[4,256,3,256]{3,2,1,0:T(4,128)(2,1)}, u32[]{:S(2)}) copy-start(bf16[4,256,3,256]{3,2,1,0:T(4,128)(2,1)} %get-tuple-element.5) | copy-start | bytes 4718596
  61.3 11.7 %collective-permute-start.4 = (bf16[3,256,512]{2,1,0:T(8,128)(2,1)S(1)}, bf16[3,256,512]{2,1,0:T(8,128)(2,1)S(1)}, u32[]{:S(2)}, u32[]{:S(2)}) collective-permute-start(bf16[3,256,512]{2,1,0:T(8,128)(2,1)S(1)} %collective-permute-done.2), channel_id=1, source_target_pairs={{0,112},{16,0},{32,16},{48,32},{64,48},{80,64},{96,80},{112,96},{1... | collective-permute-start | bytes 2359304 | tf_op jit(solution)/shard_map/ppermute | solution.py:19
  62.0 3.5 %copy-start.4 = (bf16[4,256,3,256]{3,2,1,0:T(4,128)(2,1)S(1)}, bf16[4,256,3,256]{3,2,1,0:T(4,128)(2,1)}, u32[]{:S(2)}) copy-start(bf16[4,256,3,256]{3,2,1,0:T(4,128)(2,1)} %get-tuple-element.6) | copy-start | bytes 4718596
  64.3 10.1 %collective-permute-start.6 = (bf16[3,256,512]{2,1,0:T(8,128)(2,1)S(1)}, bf16[3,256,512]{2,1,0:T(8,128)(2,1)S(1)}, u32[]{:S(2)}, u32[]{:S(2)}) collective-permute-start(bf16[3,256,512]{2,1,0:T(8,128)(2,1)S(1)} %collective-permute-done.5), channel_id=1, source_target_pairs={{0,16},{16,32},{32,48},{48,64},{64,80},{80,96},{96,112},{112,0},{1... | collective-permute-start | bytes 2359304 | tf_op jit(solution)/shard_map/ppermute | solution.py:17
  65.5 1.6 copy-start.3
  73.0 1.6 copy-start.1
  96.6 15.5 %all-to-all-start.1 = ((f32[16,32,512]{2,1,0:T(8,128)}), f32[16,32,512]{2,1,0:T(8,128)S(1)}, u32[]{:S(2)}, u32[]{:S(2)}) async-start(f32[16,32,512]{2,1,0:T(8,128)} %broadcast_in_dim.10), calls=%async_computation.1 | async-start | bytes 2097152 | tf_op jit(solution)/shard_map/all_to_all | solution.py:42
  100.2 50.6 %all-gather.7.cloned.1.call-start = ((), (), s32[]{:S(2)}) async-start(), calls=%async_computation.9 | async-start | bytes 2359296 | tf_op jit(solution)/shard_map/all_gather | solution.py:26
  113.8 99.5 %all-gather.9.cloned.1.call-start = ((), (), s32[]{:S(2)}) async-start(), calls=%async_computation.10 | async-start | bytes 2359296 | tf_op jit(solution)/shard_map/all_gather | solution.py:26
  188.2 93.5 %all-gather.11.cloned.1.call-start = ((), (), s32[]{:S(2)}) async-start(), calls=%async_computation.11 | async-start | bytes 2359296 | tf_op jit(solution)/shard_map/all_gather | solution.py:26
  237.0 18.7 %copy-start.8 = (bf16[2,256,512]{2,1,0:T(8,128)(2,1)S(1)}, bf16[2,256,512]{2,1,0:T(8,128)(2,1)}, u32[]{:S(2)}) copy-start(bf16[2,256,512]{2,1,0:T(8,128)(2,1)} %get-tuple-element.10) | copy-start | bytes 1572868
  237.1 44.6 %copy-start.9 = (bf16[1,2,256,1,256]{4,2,3,1,0:T(8,128)(2,1)S(1)}, bf16[1,2,256,1,256]{4,2,3,1,0:T(8,128)(2,1)}, u32[]{:S(2)}) copy-start(bf16[1,2,256,1,256]{4,2,3,1,0:T(8,128)(2,1)} %get-tuple-element.13) | copy-start | bytes 786436
  306.3 13.1 %all-to-all-start.7 = ((bf16[16,32,512]{2,1,0:T(8,128)(2,1)}), bf16[16,32,512]{2,1,0:T(8,128)(2,1)S(1)}, u32[]{:S(2)}, u32[]{:S(2)}) async-start(bf16[16,32,512]{2,1,0:T(8,128)(2,1)} %broadcast_in_dim.13), calls=%async_computation.7 | async-start | bytes 1048576 | tf_op jit(solution)/shard_map/all_to_all | solution.py:42
  319.5 14.0 %copy-start.2 = (bf16[4,256,512]{2,1,0:T(8,128)(2,1)}, bf16[4,256,512]{2,1,0:T(8,128)(2,1)S(1)}, u32[]{:S(2)}) copy-start(bf16[4,256,512]{2,1,0:T(8,128)(2,1)S(1)} %pad_maximum_fusion) | copy-start | bytes 3145732
  319.5 13.4 %copy-start.10 = (f32[32,512]{1,0:T(8,128)S(1)}, f32[32,512]{1,0:T(8,128)}, u32[]{:S(2)}) copy-start(f32[32,512]{1,0:T(8,128)} %param.11) | copy-start | bytes 196612
Sparse Core Ops, SparseCore 0:
  113.9 36.8 all-gather.6
  188.3 25.0 all-gather.8
  256.6 25.0 all-gather.10
